TPU v7x, 128 devices: a whole 4x4x4 slice. The times are simulated.
128 devices in a mesh: row: 16 (over y, z), col: 8 (over x, core).
Axes of the slice: x: 4, y: 4, z: 4, core: 2. Of those that a mesh axis runs over, the one named last changes fastest.
Arguments:
- matrix: float32 [18432, 18432], P('row', 'col'), as said below
Outputs:
- updated: float32 [18432, 18432], P('row', 'col')
- reflectors: float32 [18432, 512], P('row')
Inputs may be any that keep to these rules, and one draw needn't show every extreme that they name: matrix is symmetric.
All inputs are finite; a program needn't handle non-finite values.
Results may differ from a plain program's by a relative error of at most 0.00016.
Values sent between devices are 32-bit elements; how exact they have to be, the bound alone decides.
A program may use at most 128 MiB of HBM per device.

v0:
```python
import jax
import jax.numpy as jnp
from jax import lax
from jax.sharding import PartitionSpec as P

BAND = 256
PANELS = 2


def spread(array, axis, root):
    mine = lax.axis_index(axis) == root
    return lax.psum(jnp.where(mine, array, jnp.zeros_like(array)), axis)


def contract_first(left, right):
    return lax.dot_general(left, right, (((0,), (0,)), ((), ())), precision=lax.Precision.HIGHEST)


def body(matrix):
    high = lax.Precision.HIGHEST
    current = matrix
    row_count = matrix.shape[0]
    col_count = matrix.shape[1]
    row_start = lax.axis_index("row") * row_count
    col_start = lax.axis_index("col") * col_count
    row_places = row_start + jnp.arange(row_count, dtype=jnp.int32)
    col_places = col_start + jnp.arange(col_count, dtype=jnp.int32)
    columns = jnp.arange(BAND, dtype=jnp.int32)
    identity = jnp.eye(BAND, dtype=jnp.float32)
    stored = []
    history = []
    for which_panel in range(PANELS):
        start = (which_panel + 1) * BAND
        low_edge = which_panel * BAND
        high_edge = (which_panel + 1) * BAND
        local_panel = current[:, low_edge:high_edge]
        panel_rows = spread(local_panel, "col", 0)
        row_strip = spread(current[low_edge:high_edge, :], "row", 0)
        panel_rows = jnp.where(row_places[:, None] >= start, panel_rows, 0.0)
        unit_rows = (row_places[:, None] - start == columns[None, :]).astype(jnp.float32)
        gram_sum, top_block = lax.psum(
            (contract_first(panel_rows, panel_rows), contract_first(unit_rows, panel_rows)), "row"
        )
        factor_low = jnp.linalg.cholesky(gram_sum)
        rows_vec_t = (
            jax.scipy.linalg.solve_triangular(factor_low, panel_rows.T, lower=True) + unit_rows.T
        )
        q_top = jax.scipy.linalg.solve_triangular(factor_low, top_block.T, lower=True).T
        shifted = identity + q_top
        factor_two = jnp.linalg.cholesky(jnp.dot(shifted, shifted.T, precision=high))
        inner = jax.scipy.linalg.solve_triangular(factor_two, identity, lower=True)
        transform = jnp.dot(shifted.T, jnp.dot(inner.T, inner, precision=high), precision=high)
        row_strip = jnp.where(col_places[None, :] >= start, row_strip, 0.0)
        unit_cols = (columns[:, None] == col_places[None, :] - start).astype(jnp.float32)
        cols_vec_t = (
            jax.scipy.linalg.solve_triangular(factor_low, row_strip, lower=True) + unit_cols
        )
        stored.append(rows_vec_t)
        image_part = jnp.dot(rows_vec_t, current, precision=high)
        image_cols = lax.psum(image_part, "row")
        curvature = lax.psum(jnp.dot(image_cols, cols_vec_t.T, precision=high), "col")
        row_part = lax.dot_general(cols_vec_t, current, (((1,), (1,)), ((), ())), precision=high)
        image_rows = lax.psum(row_part, "col")
        middle = jnp.dot(jnp.dot(transform, curvature, precision=high), transform.T, precision=high)
        w_cols = jnp.dot(transform, image_cols, precision=high) - 0.5 * jnp.dot(
            middle.T, cols_vec_t, precision=high
        )
        w_rows = jnp.dot(transform, image_rows, precision=high) - 0.5 * jnp.dot(
            middle.T, rows_vec_t, precision=high
        )
        current = current - contract_first(rows_vec_t, w_cols) - contract_first(w_rows, cols_vec_t)
        history.append((rows_vec_t, w_rows, w_cols, cols_vec_t))
    return (current, jnp.concatenate(stored, axis=0).T)


def solution(mesh):
    placed = (P("row", "col"),)
    return jax.shard_map(
        body,
        mesh=mesh,
        in_specs=placed,
        out_specs=(P("row", "col"), P("row", None)),
        check_vma=False,
    )
```

profile of v0, /device:TPU:0, one launch (start us, length us, event | category | flops | bytes accessed | tf_op | source)
XLA Modules:
  0.0 1102.8 jit_solution(8772189510013273424)
XLA Ops:
  7.2 2.4 slice_select_fusion.3
  9.7 3.2 slice_select_fusion.1
  12.9 63.4 %all-reduce.14.cloned.1.call-done = f32[1152,256]{1,0:T(8,128)} async-done(((f32[1152,256]{1,0:T(8,128)}), f32[1152,256]{1,0:T(8,128)}) %all-reduce.14.cloned.1.call-update) | async-done | bytes 1179664 | tf_op jit(solution)/shard_map/psum | solution.py:12
  76.3 4.9 fusion.14
  82.1 2.1 fusion.8
  84.2 81.0 %all-reduce.16.cloned.1.call-done = f32[256,256]{0,1:T(8,128)} async-done(((f32[256,256]{0,1:T(8,128)}), f32[256,256]{0,1:T(8,128)}) %all-reduce.16.cloned.1.call-update) | async-done | bytes 262160 | tf_op jit(solution)/shard_map/psum | solution.py:41
  167.3 11.7 %cholesky.214 = f32[128,128]{1,0:T(8,128)S(1)} custom-call(f32[128,128]{1,0:T(8,128)S(1)} %cholesky.346), custom_call_target="Cholesky" | custom-call | tf_op jit(solution)/shard_map/jit(cholesky)/cholesky | solution.py:44
  179.0 9.8 custom-call.25
  189.4 11.7 %cholesky.231 = f32[128,128]{1,0:T(8,128)S(1)} custom-call(f32[128,128]{1,0:T(8,128)S(1)} %convolution_subtract_fusion.15), custom_call_target="Cholesky" | custom-call | tf_op jit(solution)/shard_map/jit(cholesky)/cholesky | solution.py:44
  203.2 4.1 while.16
  207.9 19.7 %custom-call.26 = f32[2,128,128]{1,2,0:T(8,128)S(1)} custom-call(f32[2,128,128]{2,1,0:T(8,128)S(1)} %get-tuple-element.60), custom_call_target="InvertDiagBlocksLowerTriangular" | custom-call | tf_op jit(solution)/shard_map/jit(_solve_triangular)/triangular_solve | solution.py:46
  230.3 13.3 %fusion.123 = f32[256,2304]{1,0:T(8,128)} fusion(f32[256,1152]{1,0:T(8,128)S(1)} %maximum_add_fusion.2, f32[1152,2304]{1,0:T(8,128)} %param.8), kind=kOutput, calls=%fused_computation.219 | convolution fusion | flops 8153726976 | bytes 14155776 | tf_op jit(solution)/shard_map/dot_general | solution.py:59
  245.0 109.0 %all-reduce.24.cloned.1.call-done = (f32[256,256]{1,0:T(8,128)}, f32[256,2304]{1,0:T(8,128)}, f32[256,2304]{1,0:T(8,128)}) async-done(((f32[256,256]{1,0:T(8,128)}, f32[256,2304]{1,0:T(8,128)}, f32[256,2304]{1,0:T(8,128)}), (f32[256,256]{1,0:T(8,128)}, f32[256,2304]{1,0:T(8,128)}, f32[256,2304]{1,0:T(8,128)})) %all-reduce.24.cloned.1.call-update) | async-done | bytes 4980752 | tf_op jit(solution)/shard_map/psum | solution.py:41
  354.0 1.8 broadcast_select_fusion.1
  359.4 14.0 %fusion.47 = f32[256,1152]{1,0:T(8,128)} fusion(f32[1152,2304]{1,0:T(8,128)} %param.8, f32[128,2304]{1,0:T(8,128)S(1)} %fusion.81, f32[128,2304]{1,0:T(8,128)S(1)} %fusion.6, s32[2304]{0:T(1024)S(1)} %fusion.95), kind=kOutput, calls=%fused_computation.106 | convolution fusion | flops 8156086272 | bytes 14164992 | tf_op jit(solution)/shard_map/dot_general | solution.py:62
  373.4 3.1 fusion.48
  382.1 1.8 copy.5
  386.2 13.2 %cholesky.248 = f32[128,128]{1,0:T(8,128)} custom-call(f32[128,128]{1,0:T(8,128)} %cholesky.349), custom_call_target="Cholesky" | custom-call | tf_op jit(solution)/shard_map/jit(cholesky)/cholesky | solution.py:50
  399.4 2.0 select_reduce_fusion.5
  403.0 11.3 %custom-call.28 = f32[1,128,128]{1,2,0:T(8,128)} custom-call(f32[1,128,128]{2,1,0:T(8,128)} %get-tuple-element.131), custom_call_target="InvertDiagBlocksLowerTriangular" | custom-call | tf_op jit(solution)/shard_map/jit(cholesky)/cholesky | solution.py:50
  414.3 1.7 constant_dynamic-update-slice_fusion.4
  416.0 1.7 convolution_subtract_fusion.14
  417.7 13.3 %cholesky.265 = f32[128,128]{1,0:T(8,128)} custom-call(f32[128,128]{1,0:T(8,128)} %convolution_subtract_fusion.14), custom_call_target="Cholesky" | custom-call | tf_op jit(solution)/shard_map/jit(cholesky)/cholesky | solution.py:50
  435.9 1.7 select_select_fusion.2
  438.2 8.3 while.17
  439.5 2.9 bitcast_dynamic-update-slice_fusion.9
  443.7 2.9 bitcast_dynamic-update-slice_fusion.9
  446.6 21.1 %custom-call.29 = f32[2,128,128]{1,2,0:T(8,128)} custom-call(f32[2,128,128]{2,1,0:T(8,128)} %get-tuple-element.62), custom_call_target="InvertDiagBlocksLowerTriangular" | custom-call | tf_op jit(solution)/shard_map/jit(_solve_triangular)/triangular_solve | solution.py:51
  469.6 2.0 convolution_subtract_fusion.10
  472.9 1.6 fusion.31
  476.6 5.2 fusion.124
  481.7 53.3 %all-reduce.28.cloned.1.call-done = (f32[256,256]{1,0:T(8,128)}, f32[256,1152]{1,0:T(8,128)}) async-done(((f32[256,256]{1,0:T(8,128)}, f32[256,1152]{1,0:T(8,128)}), (f32[256,256]{1,0:T(8,128)}, f32[256,1152]{1,0:T(8,128)})) %all-reduce.28.cloned.1.call-update) | async-done | bytes 1441808 | tf_op jit(solution)/shard_map/psum | solution.py:61
  535.0 2.6 fusion.127
  540.2 2.6 fusion.1
  542.8 12.7 %convolution_subtract_fusion.3 = f32[1152,2304]{1,0:T(8,128)S(1)} fusion(f32[1152,2304]{1,0:T(8,128)} %param.8, f32[256,1152]{1,0:T(8,128)S(1)} %maximum_add_fusion.2, f32[256,2304]{1,0:T(8,128)S(1)} %fusion.1), kind=kOutput, calls=%fused_computation.11 | convolution fusion | flops 8156381184 | bytes 24772608 | tf_op jit(solution)/shard_map/dot_general | solution.py:16
  555.4 10.0 convolution_subtract_fusion.2
  565.4 4.1 copy-done
  570.7 3.2 slice_select_fusion
  574.0 59.2 %all-reduce.18.cloned.1.call-done = f32[1152,256]{1,0:T(8,128)} async-done(((f32[1152,256]{1,0:T(8,128)}), f32[1152,256]{1,0:T(8,128)}) %all-reduce.18.cloned.1.call-update) | async-done | bytes 1179664 | tf_op jit(solution)/shard_map/psum | solution.py:12
  633.2 4.9 fusion.11
  638.8 2.2 fusion.9
  641.0 81.1 %all-reduce.20.cloned.1.call-done = f32[256,256]{0,1:T(8,128)} async-done(((f32[256,256]{0,1:T(8,128)}), f32[256,256]{0,1:T(8,128)}) %all-reduce.20.cloned.1.call-update) | async-done | bytes 262160 | tf_op jit(solution)/shard_map/psum | solution.py:41
  724.2 11.7 %cholesky.282 = f32[128,128]{1,0:T(8,128)S(1)} custom-call(f32[128,128]{1,0:T(8,128)S(1)} %cholesky.352), custom_call_target="Cholesky" | custom-call | tf_op jit(solution)/shard_map/jit(cholesky)/cholesky | solution.py:44
  735.9 9.8 custom-call.31
  746.2 11.7 %cholesky.299 = f32[128,128]{1,0:T(8,128)S(1)} custom-call(f32[128,128]{1,0:T(8,128)S(1)} %convolution_subtract_fusion.13), custom_call_target="Cholesky" | custom-call | tf_op jit(solution)/shard_map/jit(cholesky)/cholesky | solution.py:44
  760.7 4.5 while.18
  765.2 19.7 %custom-call.32 = f32[2,128,128]{1,2,0:T(8,128)S(1)} custom-call(f32[2,128,128]{2,1,0:T(8,128)S(1)} %get-tuple-element.64), custom_call_target="InvertDiagBlocksLowerTriangular" | custom-call | tf_op jit(solution)/shard_map/jit(_solve_triangular)/triangular_solve | solution.py:46
  787.6 13.7 %fusion.128 = f32[256,2304]{1,0:T(8,128)} fusion(f32[256,1152]{1,0:T(8,128)S(1)} %maximum_add_fusion.3, f32[1152,2304]{1,0:T(8,128)} %copy-done), kind=kOutput, calls=%fused_computation.224 | convolution fusion | flops 8153726976 | bytes 14155776 | tf_op jit(solution)/shard_map/dot_general | solution.py:59
  803.0 3.0 copy.9
  806.0 105.8 %all-reduce.22.cloned.1.call-done = (f32[256,256]{1,0:T(8,128)}, f32[256,2304]{1,0:T(8,128)}, f32[256,2304]{1,0:T(8,128)}) async-done(((f32[256,256]{1,0:T(8,128)}, f32[256,2304]{1,0:T(8,128)}, f32[256,2304]{1,0:T(8,128)}), (f32[256,256]{1,0:T(8,128)}, f32[256,2304]{1,0:T(8,128)}, f32[256,2304]{1,0:T(8,128)})) %all-reduce.22.cloned.1.call-update) | async-done | bytes 4980752 | tf_op jit(solution)/shard_map/psum | solution.py:41
  911.8 1.9 broadcast_select_fusion
  917.2 13.8 %fusion.45 = f32[256,1152]{1,0:T(8,128)} fusion(f32[1152,2304]{1,0:T(8,128)} %copy-done, f32[128,2304]{1,0:T(8,128)S(1)} %fusion.84, f32[128,2304]{1,0:T(8,128)S(1)} %fusion.4, s32[2304]{0:T(1024)S(1)} %fusion.93), kind=kOutput, calls=%fused_computation.104 | convolution fusion | flops 8156086272 | bytes 14164992 | tf_op jit(solution)/shard_map/dot_general | solution.py:62
  931.1 3.1 fusion.46
  936.5 11.7 %cholesky.316 = f32[128,128]{1,0:T(8,128)S(1)} custom-call(f32[128,128]{1,0:T(8,128)S(1)} %cholesky.355), custom_call_target="Cholesky" | custom-call | tf_op jit(solution)/shard_map/jit(cholesky)/cholesky | solution.py:50
  948.3 9.8 custom-call.34
  960.3 11.9 %cholesky.333 = f32[128,128]{1,0:T(8,128)S(1)} custom-call(f32[128,128]{1,0:T(8,128)S(1)} %convolution_subtract_fusion.12), custom_call_target="Cholesky" | custom-call | tf_op jit(solution)/shard_map/jit(cholesky)/cholesky | solution.py:50
  975.0 4.1 while.19
  979.1 19.7 %custom-call.35 = f32[2,128,128]{1,2,0:T(8,128)S(1)} custom-call(f32[2,128,128]{2,1,0:T(8,128)S(1)} %get-tuple-element.66), custom_call_target="InvertDiagBlocksLowerTriangular" | custom-call | tf_op jit(solution)/shard_map/jit(_solve_triangular)/triangular_solve | solution.py:51
  1000.8 5.2 fusion.129
  1006.0 56.9 %all-reduce.26.cloned.1.call-done = (f32[256,256]{1,0:T(8,128)}, f32[256,1152]{1,0:T(8,128)}) async-done(((f32[256,256]{1,0:T(8,128)}, f32[256,1152]{1,0:T(8,128)}), (f32[256,256]{1,0:T(8,128)}, f32[256,1152]{1,0:T(8,128)})) %all-reduce.26.cloned.1.call-update) | async-done | bytes 1441808 | tf_op jit(solution)/shard_map/psum | solution.py:61
  1062.9 2.6 fusion.132
  1068.4 2.5 fusion
  1070.9 12.6 %convolution_subtract_fusion.1 = f32[1152,2304]{1,0:T(8,128)S(1)} fusion(f32[1152,2304]{1,0:T(8,128)} %copy-done, f32[256,1152]{1,0:T(8,128)S(1)} %copy-done.2, f32[256,2304]{1,0:T(8,128)S(1)} %fusion), kind=kOutput, calls=%fused_computation.9 | convolution fusion | flops 8156381184 | bytes 24772608 | tf_op jit(solution)/shard_map/dot_general | solution.py:16
  1083.5 12.2 %convolution_subtract_fusion = f32[1152,2304]{1,0:T(8,128)} fusion(f32[1152,2304]{1,0:T(8,128)S(1)} %convolution_subtract_fusion.1, f32[256,1152]{1,0:T(8,128)S(1)} %fusion.2, f32[128,2304]{1,0:T(8,128)S(1)} %fusion.84, f32[128,2304]{1,0:T(8,128)S(1)} %fusion.4, s32[2304]{0:T(1024)S(1)} %fusion.93), kind=kOutput, calls=%fused_computation.8 | convolution fusion | flops 8158740480 | bytes 24781824 | tf_op jit(solution)/shard_map/dot_general | solution.py:16
  (190 shorter events, 72.9 us)
Async XLA Ops:
  7.2 69.2 %all-reduce.14.cloned.1.call-start = ((), (), s32[]{:S(2)}) async-start(), calls=%async_computation | async-start | bytes 2359296 | tf_op jit(solution)/shard_map/psum | solution.py:12
  9.6 155.6 %all-reduce.16.cloned.1.call-start = ((), (), s32[]{:S(2)}) async-start(), calls=%async_computation.1 | async-start | bytes 524288 | tf_op jit(solution)/shard_map/psum | solution.py:41
  76.3 5.5 copy-start.3
  81.3 272.7 %all-reduce.24.cloned.1.call-start = ((), (), s32[]{:S(2)}) async-start(), calls=%async_computation.5 | async-start | bytes 9961472 | tf_op jit(solution)/shard_map/psum | solution.py:41
  207.3 0.5 copy-start.28
  207.9 149.1 %copy-start.11 = (f32[256,256]{1,0:T(8,128)}, f32[256,256]{1,0:T(8,128)S(1)}, u32[]{:S(2)}) copy-start(f32[256,256]{1,0:T(8,128)S(1)} %get-tuple-element.366) | copy-start | bytes 786436
  227.6 128.3 %copy-start.16 = (f32[2,128,128]{1,2,0:T(8,128)}, f32[2,128,128]{1,2,0:T(8,128)S(1)}, u32[]{:S(2)}) copy-start(f32[2,128,128]{1,2,0:T(8,128)S(1)} %custom-call.26) | copy-start | bytes 393220
  243.6 291.5 %all-reduce.28.cloned.1.call-start = ((), (), s32[]{:S(2)}) async-start(), calls=%async_computation.7 | async-start | bytes 2883584 | tf_op jit(solution)/shard_map/psum | solution.py:61
  357.0 1.2 copy-start.17
  359.3 14.0 %copy-start.5 = (f32[256,2304]{1,0:T(8,128)S(1)}, f32[256,2304]{1,0:T(8,128)}, u32[]{:S(2)}) copy-start(f32[256,2304]{1,0:T(8,128)} %get-tuple-element.106) | copy-start | bytes 7077892
  377.7 2.4 copy-start.15
  380.1 0.7 copy-start.21
  384.9 0.7 copy-start.22
  468.9 0.7 copy-start.20
  471.6 161.6 %all-reduce.18.cloned.1.call-start = ((), (), s32[]{:S(2)}) async-start(), calls=%async_computation.2 | async-start | bytes 2359296 | tf_op jit(solution)/shard_map/psum | solution.py:12
  475.9 0.7 copy-start.9
  535.0 2.7 copy-start.10
  535.0 2.7 copy-start.24
  538.5 1.7 copy-start.7
  565.4 4.1 copy-start
  570.7 151.4 %all-reduce.20.cloned.1.call-start = ((), (), s32[]{:S(2)}) async-start(), calls=%async_computation.3 | async-start | bytes 524288 | tf_op jit(solution)/shard_map/psum | solution.py:41
  633.2 5.2 copy-start.4
  638.1 0.7 copy-start.27
  638.1 273.7 %all-reduce.22.cloned.1.call-start = ((), (), s32[]{:S(2)}) async-start(), calls=%async_computation.4 | async-start | bytes 9961472 | tf_op jit(solution)/shard_map/psum | solution.py:41
  723.1 37.6 %copy-start.29 = (s32[2,2]{1,0:T(2,128)S(1)}, s32[2,2]{1,0:T(2,128)}, u32[]{:S(2)}) copy-start(s32[2,2]{1,0:T(2,128)} %get-tuple-element.391) | copy-start | bytes 52
  765.2 21.5 %copy-start.12 = (f32[256,256]{1,0:T(8,128)}, f32[256,256]{1,0:T(8,128)S(1)}, u32[]{:S(2)}) copy-start(f32[256,256]{1,0:T(8,128)S(1)} %get-tuple-element.367) | copy-start | bytes 786436
  784.9 1.9 copy-start.18
  787.6 13.9 %copy-start.1 = (f32[256,1152]{1,0:T(8,128)}, f32[256,1152]{1,0:T(8,128)S(1)}, u32[]{:S(2)}) copy-start(f32[256,1152]{1,0:T(8,128)S(1)} %maximum_add_fusion.3) | copy-start | bytes 3538948
  801.4 261.5 %all-reduce.26.cloned.1.call-start = ((), (), s32[]{:S(2)}) async-start(), calls=%async_computation.6 | async-start | bytes 2883584 | tf_op jit(solution)/shard_map/psum | solution.py:61
  911.8 1.9 copy-start.19
  913.7 1.2 copy-start.13
  917.2 13.8 %copy-start.6 = (f32[256,2304]{1,0:T(8,128)S(1)}, f32[256,2304]{1,0:T(8,128)}, u32[]{:S(2)}) copy-start(f32[256,2304]{1,0:T(8,128)} %get-tuple-element.103) | copy-start | bytes 7077892
  931.0 3.1 copy-start.26
  935.8 0.7 copy-start.23
  948.3 50.5 %copy-start.14 = (f32[256,256]{0,1:T(8,128)S(1)}, f32[256,256]{0,1:T(8,128)}, u32[]{:S(2)}) copy-start(f32[256,256]{0,1:T(8,128)} %fusion.44) | copy-start | bytes 786436
  1062.9 2.6 copy-start.25
  1065.4 1.3 copy-start.2
  1066.7 1.7 copy-start.8
Sparse Core Ops, SparseCore 0:
  10.9 65.3 all-reduce.13
  81.4 83.7 all-reduce.15
  243.7 110.2 all-reduce.23
  471.7 63.2 all-reduce.27
  570.8 62.3 all-reduce.17
  638.2 83.7 all-reduce.19
  801.5 110.2 all-reduce.21
  999.6 63.1 all-reduce.25
where the time goes:
time: 1110 us; the launch traced here: 1100 us
  waiting for transfers between devices  610 us (55%)
  other arithmetic  249 us (22%)
  matrix products  182 us (16%)
  local copies, waits for them, and re-layouts  39.9 us (4%)
  between operations  20.6 us (2%)
    psum x4, waiting for transfers between devices, body(): lax.psum((contract_first(panel_rows, panel_rows), contract_first(unit_row...  377 us
    psum x2, waiting for transfers between devices, spread(): return lax.psum(jnp.where(mine, array, jnp.zeros_like(array)), axis)  123 us
    psum x2, waiting for transfers between devices, body(): lax.psum(jnp.dot(image_cols, cols_vec_t.T, precision=high), 'col')  110 us
    another operation x14, other arithmetic, body(): jnp.linalg.cholesky(jnp.dot(shifted, shifted.T, precision=high))  78.2 us
    another operation x13, other arithmetic, body(): factor_low = jnp.linalg.cholesky(gram_sum)  68.7 us
    dot_general x8, matrix products, contract_first(): lax.dot_general(left, right, (((0,), (0,)), ((), ())), precision=lax.Prec...  61.5 us
    another operation x4, other arithmetic, body(): inner = jax.scipy.linalg.solve_triangular(factor_two, identity, lower=True)  42.5 us
    another operation x5, other arithmetic, body(): jax.scipy.linalg.solve_triangular(factor_low, panel_rows.T, lower=True)  39.4 us
  transfers between devices with their start and end apart: 8, of which 8 were waited for; matrix products, arithmetic and copies ran while one was open for 3% of the time, Pallas kernels for 0%

commit v1 on v0

--- a/solution.py
+++ b/solution.py
@@ -58,7 +58,8 @@
         stored.append(rows_vec_t)
         image_part = jnp.dot(rows_vec_t, current, precision=high)
         image_cols = lax.psum(image_part, "row")
-        curvature = lax.psum(jnp.dot(image_cols, cols_vec_t.T, precision=high), "col")
+        chunk = jnp.dot(image_cols, cols_vec_t.T, precision=high)
+        curvature = jnp.sum(lax.all_gather(chunk, "col"), axis=0)
         row_part = lax.dot_general(cols_vec_t, current, (((1,), (1,)), ((), ())), precision=high)
         image_rows = lax.psum(row_part, "col")
         middle = jnp.dot(jnp.dot(transform, curvature, precision=high), transform.T, precision=high)

time: 1110 us -> 1020 us (0.919)
  waiting for transfers between devices: 610 us -> 510 us
    psum x2, waiting for transfers between devices: 110 us -> 0.01 us  [body(): image_rows = lax.psum(row_part, 'col')]
  transfers between devices with their start and end apart: 8 -> 10, of which waited for: 8 -> 7; matrix products, arithmetic and copies ran while one was open for 3% -> 20% of each run, Pallas kernels for 0% -> 0%
where the time goes in v1:
time: 1020 us; the launch traced here: 1010 us
  waiting for transfers between devices  510 us (50%)
  other arithmetic  253 us (25%)
  matrix products  185 us (18%)
  local copies, waits for them, and re-layouts  39.4 us (4%)
  between operations  20.4 us (2%)
    psum x4, waiting for transfers between devices, body(): lax.psum((contract_first(panel_rows, panel_rows), contract_first(unit_row...  377 us
    psum x2, waiting for transfers between devices, spread(): return lax.psum(jnp.where(mine, array, jnp.zeros_like(array)), axis)  123 us
    another operation x14, other arithmetic, body(): jnp.linalg.cholesky(jnp.dot(shifted, shifted.T, precision=high))  78.1 us
    another operation x13, other arithmetic, body(): factor_low = jnp.linalg.cholesky(gram_sum)  68.5 us
    dot_general x8, matrix products, contract_first(): lax.dot_general(left, right, (((0,), (0,)), ((), ())), precision=lax.Prec...  61.5 us
    another operation x4, other arithmetic, body(): inner = jax.scipy.linalg.solve_triangular(factor_two, identity, lower=True)  42.5 us
    another operation x5, other arithmetic, body(): jax.scipy.linalg.solve_triangular(factor_low, panel_rows.T, lower=True)  39.4 us
    dot_general x2, matrix products, body(): lax.dot_general(cols_vec_t, current, (((1,), (1,)), ((), ())), precision=...  27.2 us
  transfers between devices with their start and end apart: 10, of which 7 were waited for; matrix products, arithmetic and copies ran while one was open for 20% of the time, Pallas kernels for 0%

profile of v1, /device:TPU:0, one launch (start us, length us, event | category | flops | bytes accessed | tf_op | source)
XLA Modules:
  0.0 1010.6 jit_solution(17658977333179257208)
XLA Ops:
  7.2 2.4 slice_select_fusion.3
  9.7 3.2 slice_select_fusion.1
  12.9 63.4 %all-reduce.12.cloned.1.call-done = f32[1152,256]{1,0:T(8,128)} async-done(((f32[1152,256]{1,0:T(8,128)}), f32[1152,256]{1,0:T(8,128)}) %all-reduce.12.cloned.1.call-update) | async-done | bytes 1179664 | tf_op jit(solution)/shard_map/psum | solution.py:12
  76.3 4.9 fusion.14
  82.1 2.2 fusion.8
  84.2 81.0 %all-reduce.14.cloned.1.call-done = f32[256,256]{0,1:T(8,128)} async-done(((f32[256,256]{0,1:T(8,128)}), f32[256,256]{0,1:T(8,128)}) %all-reduce.14.cloned.1.call-update) | async-done | bytes 262160 | tf_op jit(solution)/shard_map/psum | solution.py:41
  167.3 11.7 %cholesky.214 = f32[128,128]{1,0:T(8,128)S(1)} custom-call(f32[128,128]{1,0:T(8,128)S(1)} %cholesky.346), custom_call_target="Cholesky" | custom-call | tf_op jit(solution)/shard_map/jit(cholesky)/cholesky | solution.py:44
  179.0 9.8 custom-call.25
  189.3 11.7 %cholesky.231 = f32[128,128]{1,0:T(8,128)S(1)} custom-call(f32[128,128]{1,0:T(8,128)S(1)} %convolution_subtract_fusion.15), custom_call_target="Cholesky" | custom-call | tf_op jit(solution)/shard_map/jit(cholesky)/cholesky | solution.py:44
  203.1 4.1 while.16
  207.9 19.7 %custom-call.26 = f32[2,128,128]{1,2,0:T(8,128)S(1)} custom-call(f32[2,128,128]{2,1,0:T(8,128)S(1)} %get-tuple-element.60), custom_call_target="InvertDiagBlocksLowerTriangular" | custom-call | tf_op jit(solution)/shard_map/jit(_solve_triangular)/triangular_solve | solution.py:46
  230.2 13.3 %fusion.123 = f32[256,2304]{1,0:T(8,128)} fusion(f32[256,1152]{1,0:T(8,128)S(1)} %maximum_add_fusion.2, f32[1152,2304]{1,0:T(8,128)} %param.8), kind=kOutput, calls=%fused_computation.219 | convolution fusion | flops 8153726976 | bytes 14155776 | tf_op jit(solution)/shard_map/dot_general | solution.py:59
  244.9 109.0 %all-reduce.26.cloned.1.call-done = (f32[256,256]{1,0:T(8,128)}, f32[256,2304]{1,0:T(8,128)}, f32[256,2304]{1,0:T(8,128)}) async-done(((f32[256,256]{1,0:T(8,128)}, f32[256,2304]{1,0:T(8,128)}, f32[256,2304]{1,0:T(8,128)}), (f32[256,256]{1,0:T(8,128)}, f32[256,2304]{1,0:T(8,128)}, f32[256,2304]{1,0:T(8,128)})) %all-reduce.26.cloned.1.call-update) | async-done | bytes 4980752 | tf_op jit(solution)/shard_map/psum | solution.py:41
  354.0 1.8 broadcast_select_fusion.1
  359.3 13.7 %fusion.47 = f32[256,1152]{1,0:T(8,128)} fusion(f32[1152,2304]{1,0:T(8,128)} %param.8, f32[128,2304]{1,0:T(8,128)S(1)} %fusion.81, f32[128,2304]{1,0:T(8,128)S(1)} %fusion.6, s32[2304]{0:T(1024)S(1)} %fusion.95), kind=kOutput, calls=%fused_computation.106 | convolution fusion | flops 8156086272 | bytes 14164992 | tf_op jit(solution)/shard_map/dot_general | solution.py:63
  378.7 1.8 copy.5
  380.5 4.7 fusion.48
  388.1 13.2 %cholesky.248 = f32[128,128]{1,0:T(8,128)} custom-call(f32[128,128]{1,0:T(8,128)} %cholesky.349), custom_call_target="Cholesky" | custom-call | tf_op jit(solution)/shard_map/jit(cholesky)/cholesky | solution.py:50
  402.9 2.0 select_reduce_fusion.5
  404.9 11.3 %custom-call.28 = f32[1,128,128]{1,2,0:T(8,128)} custom-call(f32[1,128,128]{2,1,0:T(8,128)} %get-tuple-element.127), custom_call_target="InvertDiagBlocksLowerTriangular" | custom-call | tf_op jit(solution)/shard_map/jit(cholesky)/cholesky | solution.py:50
  416.2 1.7 constant_dynamic-update-slice_fusion.4
  417.9 1.7 convolution_subtract_fusion.14
  419.6 13.2 %cholesky.265 = f32[128,128]{1,0:T(8,128)} custom-call(f32[128,128]{1,0:T(8,128)} %convolution_subtract_fusion.14), custom_call_target="Cholesky" | custom-call | tf_op jit(solution)/shard_map/jit(cholesky)/cholesky | solution.py:50
  437.7 1.7 select_select_fusion.2
  440.1 8.6 while.17
  441.5 2.9 bitcast_dynamic-update-slice_fusion.9
  445.8 2.9 bitcast_dynamic-update-slice_fusion.9
  448.7 21.1 %custom-call.29 = f32[2,128,128]{1,2,0:T(8,128)} custom-call(f32[2,128,128]{2,1,0:T(8,128)} %get-tuple-element.62), custom_call_target="InvertDiagBlocksLowerTriangular" | custom-call | tf_op jit(solution)/shard_map/jit(_solve_triangular)/triangular_solve | solution.py:51
  476.4 3.5 fusion.124
  479.9 3.6 fusion.127
  483.5 2.5 reduce_sum.18
  490.6 2.6 fusion.1
  493.1 12.7 %convolution_subtract_fusion.3 = f32[1152,2304]{1,0:T(8,128)S(1)} fusion(f32[1152,2304]{1,0:T(8,128)} %param.8, f32[256,1152]{1,0:T(8,128)S(1)} %maximum_add_fusion.2, f32[256,2304]{1,0:T(8,128)S(1)} %fusion.1), kind=kOutput, calls=%fused_computation.11 | convolution fusion | flops 8156381184 | bytes 24772608 | tf_op jit(solution)/shard_map/dot_general | solution.py:16
  505.8 10.0 convolution_subtract_fusion.2
  515.8 4.1 copy-done
  521.1 3.2 slice_select_fusion
  524.3 59.3 %all-reduce.18.cloned.1.call-done = f32[1152,256]{1,0:T(8,128)} async-done(((f32[1152,256]{1,0:T(8,128)}), f32[1152,256]{1,0:T(8,128)}) %all-reduce.18.cloned.1.call-update) | async-done | bytes 1179664 | tf_op jit(solution)/shard_map/psum | solution.py:12
  583.7 4.9 fusion.11
  589.3 2.2 fusion.9
  591.4 81.1 %all-reduce.20.cloned.1.call-done = f32[256,256]{0,1:T(8,128)} async-done(((f32[256,256]{0,1:T(8,128)}), f32[256,256]{0,1:T(8,128)}) %all-reduce.20.cloned.1.call-update) | async-done | bytes 262160 | tf_op jit(solution)/shard_map/psum | solution.py:41
  674.6 11.7 %cholesky.282 = f32[128,128]{1,0:T(8,128)S(1)} custom-call(f32[128,128]{1,0:T(8,128)S(1)} %cholesky.352), custom_call_target="Cholesky" | custom-call | tf_op jit(solution)/shard_map/jit(cholesky)/cholesky | solution.py:44
  686.4 9.8 custom-call.31
  696.7 11.7 %cholesky.299 = f32[128,128]{1,0:T(8,128)S(1)} custom-call(f32[128,128]{1,0:T(8,128)S(1)} %convolution_subtract_fusion.13), custom_call_target="Cholesky" | custom-call | tf_op jit(solution)/shard_map/jit(cholesky)/cholesky | solution.py:44
  711.0 4.4 while.18
  715.4 19.7 %custom-call.32 = f32[2,128,128]{1,2,0:T(8,128)S(1)} custom-call(f32[2,128,128]{2,1,0:T(8,128)S(1)} %get-tuple-element.64), custom_call_target="InvertDiagBlocksLowerTriangular" | custom-call | tf_op jit(solution)/shard_map/jit(_solve_triangular)/triangular_solve | solution.py:46
  737.8 13.7 %fusion.128 = f32[256,2304]{1,0:T(8,128)} fusion(f32[256,1152]{1,0:T(8,128)S(1)} %maximum_add_fusion.3, f32[1152,2304]{1,0:T(8,128)} %copy-done), kind=kOutput, calls=%fused_computation.224 | convolution fusion | flops 8153726976 | bytes 14155776 | tf_op jit(solution)/shard_map/dot_general | solution.py:59
  753.2 3.0 copy.9
  756.3 105.8 %all-reduce.24.cloned.1.call-done = (f32[256,256]{1,0:T(8,128)}, f32[256,2304]{1,0:T(8,128)}, f32[256,2304]{1,0:T(8,128)}) async-done(((f32[256,256]{1,0:T(8,128)}, f32[256,2304]{1,0:T(8,128)}, f32[256,2304]{1,0:T(8,128)}), (f32[256,256]{1,0:T(8,128)}, f32[256,2304]{1,0:T(8,128)}, f32[256,2304]{1,0:T(8,128)})) %all-reduce.24.cloned.1.call-update) | async-done | bytes 4980752 | tf_op jit(solution)/shard_map/psum | solution.py:41
  862.1 1.9 broadcast_select_fusion
  867.4 13.5 %fusion.45 = f32[256,1152]{1,0:T(8,128)} fusion(f32[1152,2304]{1,0:T(8,128)} %copy-done, f32[128,2304]{1,0:T(8,128)S(1)} %fusion.84, f32[128,2304]{1,0:T(8,128)S(1)} %fusion.4, s32[2304]{0:T(1024)S(1)} %fusion.93), kind=kOutput, calls=%fused_computation.104 | convolution fusion | flops 8156086272 | bytes 14164992 | tf_op jit(solution)/shard_map/dot_general | solution.py:63
  883.5 4.7 fusion.46
  889.0 11.7 %cholesky.316 = f32[128,128]{1,0:T(8,128)S(1)} custom-call(f32[128,128]{1,0:T(8,128)S(1)} %cholesky.355), custom_call_target="Cholesky" | custom-call | tf_op jit(solution)/shard_map/jit(cholesky)/cholesky | solution.py:50
  900.8 9.8 custom-call.34
  912.8 11.9 %cholesky.333 = f32[128,128]{1,0:T(8,128)S(1)} custom-call(f32[128,128]{1,0:T(8,128)S(1)} %convolution_subtract_fusion.12), custom_call_target="Cholesky" | custom-call | tf_op jit(solution)/shard_map/jit(cholesky)/cholesky | solution.py:50
  927.3 3.8 while.19
  931.1 19.7 %custom-call.35 = f32[2,128,128]{1,2,0:T(8,128)S(1)} custom-call(f32[2,128,128]{2,1,0:T(8,128)S(1)} %get-tuple-element.66), custom_call_target="InvertDiagBlocksLowerTriangular" | custom-call | tf_op jit(solution)/shard_map/jit(_solve_triangular)/triangular_solve | solution.py:51
  952.9 3.5 fusion.129
  956.4 3.6 fusion.132
  960.0 10.4 %all-gather.7.cloned.1.call-done = f32[2048,256]{1,0:T(8,128)} async-done(((f32[256,256]{1,0:T(8,128)}), f32[2048,256]{1,0:T(8,128)}) %all-gather.7.cloned.1.call-update) | async-done | bytes 2097168 | tf_op jit(solution)/shard_map/all_gather | solution.py:62
  970.4 1.8 reduce_sum.19
  973.4 2.7 fusion.2
  976.2 2.5 fusion
  978.7 12.6 %convolution_subtract_fusion.1 = f32[1152,2304]{1,0:T(8,128)S(1)} fusion(f32[1152,2304]{1,0:T(8,128)} %copy-done, f32[256,1152]{1,0:T(8,128)S(1)} %copy-done.2, f32[256,2304]{1,0:T(8,128)S(1)} %fusion), kind=kOutput, calls=%fused_computation.9 | convolution fusion | flops 8156381184 | bytes 24772608 | tf_op jit(solution)/shard_map/dot_general | solution.py:16
  991.3 12.2 %convolution_subtract_fusion = f32[1152,2304]{1,0:T(8,128)} fusion(f32[1152,2304]{1,0:T(8,128)S(1)} %convolution_subtract_fusion.1, f32[256,1152]{1,0:T(8,128)S(1)} %fusion.2, f32[128,2304]{1,0:T(8,128)S(1)} %fusion.84, f32[128,2304]{1,0:T(8,128)S(1)} %fusion.4, s32[2304]{0:T(1024)S(1)} %fusion.93), kind=kOutput, calls=%fused_computation.8 | convolution fusion | flops 8158740480 | bytes 24781824 | tf_op jit(solution)/shard_map/dot_general | solution.py:16
  (192 shorter events, 75.7 us)
Async XLA Ops:
  7.2 69.2 %all-reduce.12.cloned.1.call-start = ((), (), s32[]{:S(2)}) async-start(), calls=%async_computation | async-start | bytes 2359296 | tf_op jit(solution)/shard_map/psum | solution.py:12
  9.6 155.6 %all-reduce.14.cloned.1.call-start = ((), (), s32[]{:S(2)}) async-start(), calls=%async_computation.1 | async-start | bytes 524288 | tf_op jit(solution)/shard_map/psum | solution.py:41
  76.3 5.5 copy-start.3
  81.2 272.7 %all-reduce.26.cloned.1.call-start = ((), (), s32[]{:S(2)}) async-start(), calls=%async_computation.9 | async-start | bytes 9961472 | tf_op jit(solution)/shard_map/psum | solution.py:41
  207.3 0.6 copy-start.25
  207.9 149.1 %copy-start.11 = (f32[256,256]{1,0:T(8,128)}, f32[256,256]{1,0:T(8,128)S(1)}, u32[]{:S(2)}) copy-start(f32[256,256]{1,0:T(8,128)S(1)} %get-tuple-element.358) | copy-start | bytes 786436
  227.5 128.3 %copy-start.16 = (f32[2,128,128]{1,2,0:T(8,128)}, f32[2,128,128]{1,2,0:T(8,128)S(1)}, u32[]{:S(2)}) copy-start(f32[2,128,128]{1,2,0:T(8,128)S(1)} %custom-call.26) | copy-start | bytes 393220
  243.5 236.4 %all-reduce.16.cloned.1.call-start = ((), (), s32[]{:S(2)}) async-start(), calls=%async_computation.2 | async-start | bytes 2359296 | tf_op jit(solution)/shard_map/psum | solution.py:64
  357.0 1.2 copy-start.17
  373.0 110.5 %all-gather.5.cloned.1.call-start = ((), (), s32[]{:S(2)}) async-start(), calls=%async_computation.6 | async-start | bytes 2359296 | tf_op jit(solution)/shard_map/all_gather | solution.py:62
  374.3 2.4 copy-start.15
  376.8 0.7 copy-start.20
  385.3 198.4 %all-reduce.18.cloned.1.call-start = ((), (), s32[]{:S(2)}) async-start(), calls=%async_computation.3 | async-start | bytes 2359296 | tf_op jit(solution)/shard_map/psum | solution.py:12
  386.8 0.7 copy-start.21
  469.8 6.6 copy-start.5
  475.7 0.7 copy-start.9
  486.0 2.9 copy-start.10
  488.9 1.7 copy-start.8
  515.8 4.1 copy-start
  521.1 151.4 %all-reduce.20.cloned.1.call-start = ((), (), s32[]{:S(2)}) async-start(), calls=%async_computation.4 | async-start | bytes 524288 | tf_op jit(solution)/shard_map/psum | solution.py:41
  583.7 5.1 copy-start.4
  588.6 0.7 copy-start.24
  588.6 273.5 %all-reduce.24.cloned.1.call-start = ((), (), s32[]{:S(2)}) async-start(), calls=%async_computation.8 | async-start | bytes 9961472 | tf_op jit(solution)/shard_map/psum | solution.py:41
  673.6 37.5 %copy-start.26 = (s32[2,2]{1,0:T(2,128)S(1)}, s32[2,2]{1,0:T(2,128)}, u32[]{:S(2)}) copy-start(s32[2,2]{1,0:T(2,128)} %get-tuple-element.383) | copy-start | bytes 52
  715.4 21.5 %copy-start.12 = (f32[256,256]{1,0:T(8,128)}, f32[256,256]{1,0:T(8,128)S(1)}, u32[]{:S(2)}) copy-start(f32[256,256]{1,0:T(8,128)S(1)} %get-tuple-element.359) | copy-start | bytes 786436
  735.1 1.9 copy-start.18
  737.8 13.8 %copy-start.1 = (f32[256,1152]{1,0:T(8,128)}, f32[256,1152]{1,0:T(8,128)S(1)}, u32[]{:S(2)}) copy-start(f32[256,1152]{1,0:T(8,128)S(1)} %maximum_add_fusion.3) | copy-start | bytes 3538948
  751.6 204.8 %all-reduce.22.cloned.1.call-start = ((), (), s32[]{:S(2)}) async-start(), calls=%async_computation.5 | async-start | bytes 2359296 | tf_op jit(solution)/shard_map/psum | solution.py:64
  862.1 1.9 copy-start.19
  863.9 1.2 copy-start.13
  880.9 0.9 copy-start.23
  881.0 89.5 %all-gather.7.cloned.1.call-start = ((), (), s32[]{:S(2)}) async-start(), calls=%async_computation.7 | async-start | bytes 2359296 | tf_op jit(solution)/shard_map/all_gather | solution.py:62
  888.3 0.7 copy-start.22
  900.8 50.1 %copy-start.14 = (f32[256,256]{0,1:T(8,128)S(1)}, f32[256,256]{0,1:T(8,128)}, u32[]{:S(2)}) copy-start(f32[256,256]{0,1:T(8,128)} %fusion.44) | copy-start | bytes 786436
  950.8 2.0 copy-start.6
  972.2 1.3 copy-start.2
  973.4 2.7 copy-start.7
Sparse Core Ops, SparseCore 0:
  10.9 65.3 all-reduce.11
  81.4 83.7 all-reduce.13
  243.6 110.2 all-reduce.25
  373.1 63.0 all-reduce.15
  437.8 24.5 all-gather.4
  521.2 62.4 all-reduce.17
  588.7 83.7 all-reduce.19
  751.7 110.2 all-reduce.23
  881.1 63.2 all-reduce.21
  945.9 24.4 all-gather.6
